TPU v7x, 512 devices: a whole 4x4x16 slice. The times are simulated.
512 devices in a mesh: pulse: 4 (over z_lo), range: 4 (over y), tile: 32 (over z_hi, x, core).
Axes of the slice: x: 4, y: 4, z: 16 (z_hi: 4, z_lo: 4; z = z_hi * 4 + z_lo), core: 2. Of those that a mesh axis runs over, the one named last changes fastest.
Arguments:
- echo: bfloat16 [2, 1024, 32768], P(None, ('pulse', 'tile'), 'range'), may hold values from -6 to 6
- replica: bfloat16 [2, 4096], replicated, may hold values from -0.09375 to 0.09375
- interp: bfloat16 [32, 256, 128], P('range'), may hold values from -0.375 to 0.375
- band_start: int32 [1024, 32, 4], P(('pulse', 'tile'), None, 'range'), may hold values from 0 to 7040, as said below
- visible: int32 [1024, 32], P(('pulse', 'tile')), may hold values 0 or 1
- doppler: int32 [1024], P(('pulse', 'tile')), may hold values from 0 to 8191
- range_step: int32 [1024], P(('pulse', 'tile')), may hold values from 0 to 4095
Outputs:
- image: float32 [2, 8192, 4096], P(None, ('tile', 'pulse'), 'range')
Inputs may be any that keep to these rules, and one draw needn't show every extreme that they name: band_start is counted within the 8192 bins of range block b and is a multiple of 128; the values 0 and 7040 both occur.
All inputs are finite; a program needn't handle non-finite values. No bound on the sum of `visible` on one device may be relied on, other than what follows from the above.
Results may differ from a plain program's by a relative error of at most 0.0047.
Values may be sent and summed in bfloat16 or wider, within the bound.
No kernel may reach another device: no remote copies, remote signals or barrier semaphores. Data moves between devices by JAX's collectives and lax.ppermute only.
A program may use at most 64 MiB of HBM per device.

v0:
```python
import math
import jax
import jax.numpy as jnp
from jax import lax
from jax.sharding import PartitionSpec as P

AZ_DEV = 64


def padded_2(cells, sides, width):
    for axis, dim in sides:
        count = lax.axis_size(axis)
        ends = count - 1
        head = lax.slice_in_dim(cells, 0, width, axis=dim)
        tail = lax.slice_in_dim(cells, cells.shape[dim] - width, cells.shape[dim], axis=dim)
        cells = jnp.concatenate(
            [
                lax.ppermute(tail, axis, [(i, (i + 1) % count) for i in range(ends)]),
                cells,
                lax.ppermute(head, axis, [((i + 1) % count, i) for i in range(ends)]),
            ],
            axis=dim,
        )
    return cells


def toeplitz_block(padded, offset, block_width):
    segment = lax.dynamic_slice_in_dim(padded, offset, 2 * block_width + 1)
    repeated = jnp.tile(segment, block_width)[: 2 * block_width * block_width]
    skewed = repeated.reshape(block_width, 2 * block_width)
    return skewed[:, block_width:].T


def chirp_matrix(padded_real, padded_imag, offset, block_width):
    toep_real = toeplitz_block(padded_real, offset, block_width)
    toep_imag = toeplitz_block(padded_imag, offset, block_width)
    upper_rows = jnp.concatenate([toep_real, -toep_imag], axis=1)
    lower_rows = jnp.concatenate([toep_imag, toep_real], axis=1)
    return jnp.concatenate([upper_rows, lower_rows], axis=0)


def compress(extended, replica, block_width):
    chirp_len = replica.shape[1]
    pulses = extended.shape[1]
    total_blocks = extended.shape[2] // block_width
    out_blocks = total_blocks - chirp_len // block_width
    arranged = extended.reshape(2, pulses, total_blocks, block_width).transpose(1, 2, 0, 3)
    margin = jnp.zeros((2, block_width), replica.dtype)
    padded = jnp.concatenate([margin, replica, margin, margin[:, :1]], axis=1)

    def add_turn(turn_index, running):
        offset = (turn_index * block_width).astype(jnp.int32)
        matrix = chirp_matrix(padded[0], padded[1], offset, block_width)
        window = lax.dynamic_slice_in_dim(arranged, turn_index.astype(jnp.int32), out_blocks, 1)
        window = window.reshape(pulses * out_blocks, 2 * block_width)
        return running + jnp.dot(window, matrix, preferred_element_type=jnp.float32)

    start_total = jnp.zeros((pulses * out_blocks, 2 * block_width), jnp.float32)
    running = lax.fori_loop(0, chirp_len // block_width + 1, add_turn, start_total)
    shaped = running.reshape(pulses, out_blocks, 2, block_width).transpose(0, 2, 1, 3)
    return shaped.reshape(pulses, 2, out_blocks * block_width).astype(jnp.bfloat16)


def select_bands(signals, first_bins, band_len, line_block):
    pulses = signals.shape[0]
    block_total = signals.shape[2] // line_block
    band_blocks = band_len // line_block
    pieces = signals.reshape(pulses, 2, block_total, line_block)
    wanted = first_bins[:, None] // line_block + jnp.arange(band_blocks, dtype=jnp.int32)[None, :]
    chooser = (
        wanted[:, :, None] == jnp.arange(block_total, dtype=jnp.int32)[None, None, :]
    ).astype(jnp.bfloat16)
    picked = jnp.einsum("pjk,pckl->pcjl", chooser, pieces, preferred_element_type=jnp.float32)
    return picked.astype(jnp.bfloat16).reshape(pulses, 2, band_len)


def steer_lines(band_rows, interp_block, range_steps, first_line, range_total):
    pulses = band_rows.shape[0]
    block_count = interp_block.shape[0]
    line_block = interp_block.shape[2]
    pieces = band_rows.reshape(pulses, 2, block_count + 1, line_block)
    windows = jnp.concatenate([pieces[:, :, :-1], pieces[:, :, 1:]], axis=3)
    line_values = jnp.einsum(
        "pcjb,jbl->pcjl", windows, interp_block, preferred_element_type=jnp.float32
    )
    line_values = line_values.reshape(pulses, 2, block_count * line_block)
    line_number = first_line + jnp.arange(block_count * line_block, dtype=jnp.int32)
    phase_turns = range_steps[:, None] * line_number[None, :] % range_total
    phase_angle = phase_turns.astype(jnp.float32) * (2.0 * math.pi / range_total)
    cosine = jnp.cos(phase_angle)
    sine_part = jnp.sin(phase_angle)
    steered_real = line_values[:, 0] * cosine - line_values[:, 1] * sine_part
    steered_imag = line_values[:, 0] * sine_part + line_values[:, 1] * cosine
    return jnp.stack([steered_real, steered_imag], axis=1).astype(jnp.bfloat16)


def azimuth_factor(doppler_bins, visible_flags, line_number, azimuth_total, norm_scale):
    phase_turns = line_number[:, None] * doppler_bins[None, :] % azimuth_total
    phase_angle = phase_turns.astype(jnp.float32) * (2.0 * math.pi / azimuth_total)
    weight = visible_flags.astype(jnp.float32)[None, :] * norm_scale
    factor_real = (jnp.cos(phase_angle) * weight).astype(jnp.bfloat16)
    factor_imag = (jnp.sin(phase_angle) * weight).astype(jnp.bfloat16)
    return (factor_real, factor_imag)


def add_pulses(factor_real, factor_imag, steered):
    left_side = jnp.concatenate([factor_real, factor_imag], axis=1)
    steer_real = steered[:, 0]
    steer_imag = steered[:, 1]
    top_rows = jnp.concatenate([steer_real, steer_imag], axis=1)
    bottom_rows = jnp.concatenate([-steer_imag, steer_real], axis=1)
    right_side = jnp.concatenate([top_rows, bottom_rows], axis=0)
    return jnp.dot(left_side, right_side, preferred_element_type=jnp.float32)


def local(echo, replica, interp, band_start, visible, doppler, range_step):
    chirp_len = replica.shape[1]
    half_chirp = chirp_len // 2
    block_width = min(256, half_chirp)
    pulses_dev = echo.shape[1]
    line_block = interp.shape[2]
    lines_dev = interp.shape[0] * line_block
    band_len = lines_dev + line_block
    tile_count = lax.axis_size("tile")
    pulse_count = lax.axis_size("pulse")
    range_total = lines_dev * lax.axis_size("range")
    azimuth_total = AZ_DEV * pulse_count * tile_count
    group_pulses = pulses_dev * tile_count
    norm_scale = (pulses_dev * pulse_count * tile_count) ** (-0.5)
    tile_number = lax.axis_index("tile")
    first_line = lax.axis_index("range") * lines_dev
    extended = padded_2(echo, (("range", 2),), half_chirp)
    compressed = compress(extended, replica, block_width)
    empty_index = jnp.zeros((group_pulses,), jnp.int32)
    first_row = jnp.int32(0)
    signals = lax.all_gather(compressed, "tile", axis=0, tiled=True)
    starts_in = lax.all_gather(band_start, "tile", axis=0, tiled=True)
    flags_in = lax.all_gather(visible, "tile", axis=0, tiled=True)
    doppler_in = lax.all_gather(doppler, "tile", axis=0, tiled=True)
    steps_in = lax.all_gather(range_step, "tile", axis=0, tiled=True)
    first_bins = lax.dynamic_index_in_dim(starts_in[:, :, 0], tile_number, 1, keepdims=False)
    flags_tile = lax.dynamic_index_in_dim(flags_in, tile_number, 1, keepdims=False)
    band_rows = select_bands(signals, first_bins, band_len, line_block)
    steered_in = steer_lines(band_rows, interp, steps_in, first_line, range_total)
    doppler_all = lax.dynamic_update_slice_in_dim(empty_index, doppler_in, first_row, 0)
    flags_all = lax.dynamic_update_slice_in_dim(empty_index, flags_tile, first_row, 0)
    tile_first = tile_number * (pulse_count * AZ_DEV)
    strip_lines = tile_first + jnp.arange(pulse_count * AZ_DEV, dtype=jnp.int32)
    factor_real, factor_imag = azimuth_factor(
        doppler_all, flags_all, strip_lines, azimuth_total, norm_scale
    )
    partial_image = add_pulses(factor_real, factor_imag, steered_in)
    image_rows = lax.psum_scatter(partial_image, "pulse", scatter_dimension=0, tiled=True)
    return image_rows.reshape(AZ_DEV, 2, lines_dev).transpose(1, 0, 2)


def solution(mesh):
    in_specs = (
        P(None, ("pulse", "tile"), "range"),
        P(),
        P("range", None, None),
        P(("pulse", "tile"), None, "range"),
        P(("pulse", "tile"), None),
        P(("pulse", "tile")),
        P(("pulse", "tile")),
    )
    out_specs = P(None, ("tile", "pulse"), "range")
    return jax.shard_map(local, mesh=mesh, in_specs=in_specs, out_specs=out_specs, check_vma=False)
```

profile of v0, /device:TPU:1, one launch (start us, length us, event | category | flops | bytes accessed | tf_op | source)
XLA Modules:
  0.0 323.4 jit_solution(15231582714423784350)
XLA Ops:
  6.5 0.9 fusion.47
  7.5 1.3 collective-permute-start.1
  8.8 4.7 %collective-permute-start = (bf16[2,8,2048]{2,1,0:T(8,128)(2,1)S(1)}, bf16[2,8,2048]{2,1,0:T(8,128)(2,1)S(1)}, u32[]{:S(2)}, u32[]{:S(2)}) collective-permute-start(bf16[2,8,2048]{2,1,0:T(8,128)(2,1)S(1)} %get-tuple-element.126), channel_id=1, source_target_pairs={{0,32},{32,64},{64,96},{1,33},{33,65},{65,97},{2,34},{34,66},{66,9... | collective-permute-start | bytes 196616 | tf_op jit(solution)/shard_map/ppermute | solution.py:18
  13.5 0.7 maximum_maximum_fusion
  14.8 1.0 pad_maximum_fusion.1
  15.8 45.2 %while.14 = (s32[]{:T(128)}, f32[256,512]{1,0:T(8,128)S(1)}, bf16[8,48,2,256]{3,1,0,2:T(8,128)(2,1)S(1)}, bf16[2,4609]{1,0:T(2,128)(2,1)S(1)}, s32[]{:T(128)}, /*index=5*/s32[]{:T(128)}, s32[]{:T(128)}, s32[]{:T(128)}) while((s32[]{:T(128)}, f32[256,512]{1,0:T(8,128)S(1)}, bf16[8,48,2,256]{3,1,0,2:T(8,128)(2,1)S(1)}, ...), condition=%wide.region_1.0_spmd.clone, body=%wide.region_0.0_spmd.clone.sunk | while | flops 136642560 | bytes 7779505 | solution.py:59
  16.4 0.6 tile.65
  17.2 0.6 tile.67
  19.0 0.6 tile.65
  19.9 0.6 tile.67
  21.7 0.6 tile.65
  22.6 0.6 tile.67
  24.4 0.6 tile.65
  25.2 0.6 tile.67
  27.0 0.6 tile.65
  27.9 0.6 tile.67
  29.7 0.6 tile.65
  30.5 0.6 tile.67
  32.3 0.6 tile.65
  33.2 0.6 tile.67
  35.0 0.6 tile.65
  35.9 0.6 tile.67
  37.7 0.6 tile.65
  38.5 0.6 tile.67
  40.3 0.6 tile.65
  45.6 0.6 tile.65
  48.3 0.6 tile.65
  51.0 0.6 tile.65
  51.8 0.6 tile.67
  53.6 0.6 tile.65
  54.5 0.6 tile.67
  57.1 0.6 tile.67
  59.8 0.6 tile.67
  61.3 0.8 convert_element_type.58
  62.1 1.2 dynamic-slice.7
  64.4 26.6 %all-reduce.2 = (s32[256]{0:T(256)S(1)}, s32[256]{0:T(256)S(1)}) all-reduce(s32[256]{0:T(256)S(1)} %dynamic-update-slice.1, s32[256]{0:T(256)S(1)} %dynamic-update-slice), channel_id=1, replica_groups=mesh['pulse'=4,'range'=4,'tile'=32] {'tile'}, use_global_device_ids=true, to_apply=%add.1 | all-reduce | flops 512 | bytes 4096
  91.0 53.7 %all_gather.16 = s32[256,32]{1,0:T(8,128)S(1)} all-gather(s32[8,32]{1,0:T(8,128)S(1)} %copy-done.1), channel_id=1, replica_groups=mesh['pulse'=4,'range'=4,'tile'=32] {'tile'}, dimensions={0}, use_global_device_ids=true | all-gather | bytes 33792 | tf_op jit(solution)/shard_map/all_gather | solution.py:138
  144.9 74.4 %all_gather.18 = s32[256,32,1]{1,2,0:T(1,128)S(1)} all-gather(s32[8,32,1]{1,2,0:T(1,128)S(1)} %copy-done.2), channel_id=1, replica_groups=mesh['pulse'=4,'range'=4,'tile'=32] {'tile'}, dimensions={0}, use_global_device_ids=true | all-gather | bytes 33792 | tf_op jit(solution)/shard_map/all_gather | solution.py:137
  219.3 5.0 %dynamic-slice_reduce_fusion.2 = s32[256]{0:T(256)S(1)} fusion(s32[256,32,1]{1,2,0:T(1,128)S(1)} %all_gather.18, s32[]{:T(128)S(6)} %select_n.53), kind=kLoop, calls=%fused_computation.65 | loop fusion | bytes 2052 | tf_op jit(solution)/shard_map/jit(dynamic_index_in_dim)/dynamic_slice | solution.py:141
  224.4 1.3 multiply_convert_fusion.1
  225.7 14.6 %reshape.259 = bf16[256,2,64,128]{3,2,1,0:T(8,128)(2,1)} reshape(bf16[256,2,8192]{2,1,0:T(2,128)(2,1)} %all-gather.2.cloned.1.call-done) | data formatting | bytes 16777216 | tf_op jit(solution)/shard_map/reshape | solution.py:68
  240.3 4.2 %convert_bitcast_fusion = bf16[256,2,9,128]{3,2,1,0:T(8,128)(2,1)S(1)} fusion(bf16[256,2,64,128]{3,2,1,0:T(8,128)(2,1)} %reshape.259, s32[256,9]{1,0:T(8,128)S(1)} %iota_add_fusion), kind=kOutput, calls=%fused_computation.26 | convolution fusion | flops 76234752 | bytes 9577472 | tf_op jit(solution)/shard_map/pjk,pckl->pcjl/dot_general | solution.py:73
  245.2 1.3 fusion.24
  246.7 5.1 %fusion.31 = bf16[256,1024]{0,1:T(8,128)(2,1)S(1)} fusion(f32[256,2,1024]{0,2,1:T(8,128)S(1)} %bitcast.71, s32[1024]{0:T(1024)S(1)} %iota_add_fusion.1, s32[256]{0:T(256)S(1)} %get-tuple-element.116), kind=kLoop, calls=%fused_computation.42 | loop fusion | flops 4718592 | bytes 2626560 | tf_op jit(solution)/shard_map/squeeze | solution.py:108
  251.7 5.1 %fusion.43 = (bf16[256,1024]{0,1:T(8,128)(2,1)S(1)}, bf16[256,1024]{0,1:T(8,128)(2,1)S(1)}) fusion(f32[256,2,1024]{0,2,1:T(8,128)S(1)} %bitcast.72, s32[1024]{0:T(1024)S(1)} %iota_add_fusion.1, s32[256]{0:T(256)S(1)} %get-tuple-element.116), kind=kLoop, calls=%fused_computation.75 | loop fusion | flops 5505024 | bytes 3150848 | tf_op jit(solution)/shard_map/neg | solution.py:111
  256.8 2.1 fusion.9
  258.9 55.8 %reduce-scatter.2.cloned.1.call-done = f32[64,2048]{1,0:T(8,128)} async-done(((f32[256,2048]{1,0:T(8,128)}), f32[64,2048]{1,0:T(8,128)}) %reduce-scatter.2.cloned.1.call-update) | async-done | bytes 524304 | tf_op jit(solution)/shard_map/reduce_scatter | solution.py:153
  314.7 1.9 copy.49
  (298 shorter events, 29.2 us)
Async XLA Ops:
  6.5 238.6 %copy-start = (bf16[8,256,128]{2,1,0:T(8,128)(2,1)S(1)}, bf16[8,256,128]{2,1,0:T(8,128)(2,1)}, u32[]{:S(2)}) copy-start(bf16[8,256,128]{2,1,0:T(8,128)(2,1)} %param.11) | copy-start | bytes 1572868
  6.5 219.2 %all-gather.2.cloned.1.call-start = ((), (), s32[]{:S(2)}) async-start(), calls=%async_computation.1 | async-start | bytes 8650752 | tf_op jit(solution)/shard_map/all_gather | solution.py:136
  7.5 6.8 %collective-permute-start.1 = (bf16[2,8,2048]{2,1,0:T(8,128)(2,1)S(1)}, bf16[2,8,2048]{2,1,0:T(8,128)(2,1)S(1)}, u32[]{:S(2)}, u32[]{:S(2)}) collective-permute-start(bf16[2,8,2048]{2,1,0:T(8,128)(2,1)S(1)} %get-tuple-element.127), channel_id=1, source_target_pairs={{32,0},{64,32},{96,64},{33,1},{65,33},{97,65},{34,2},{66,34},{98,6... | collective-permute-start | bytes 196616 | tf_op jit(solution)/shard_map/ppermute | solution.py:20
  8.8 6.0 %collective-permute-start = (bf16[2,8,2048]{2,1,0:T(8,128)(2,1)S(1)}, bf16[2,8,2048]{2,1,0:T(8,128)(2,1)S(1)}, u32[]{:S(2)}, u32[]{:S(2)}) collective-permute-start(bf16[2,8,2048]{2,1,0:T(8,128)(2,1)S(1)} %get-tuple-element.126), channel_id=1, source_target_pairs={{0,32},{32,64},{64,96},{1,33},{33,65},{65,97},{2,34},{34,66},{66,9... | collective-permute-start | bytes 196616 | tf_op jit(solution)/shard_map/ppermute | solution.py:18
  61.1 2.9 copy-start.3
  61.1 3.1 copy-start.4
  61.1 29.9 %copy-start.1 = (s32[8,32]{1,0:T(8,128)S(1)}, s32[8,32]{1,0:T(8,128)}, u32[]{:S(2)}) copy-start(s32[8,32]{1,0:T(8,128)} %param.13) | copy-start | bytes 3076
  61.1 83.8 %copy-start.2 = (s32[8,32,1]{1,2,0:T(1,128)S(1)}, s32[8,32,1]{1,2,0:T(1,128)}, u32[]{:S(2)}) copy-start(s32[8,32,1]{1,2,0:T(1,128)} %param.12) | copy-start | bytes 3076
  62.1 252.6 %reduce-scatter.2.cloned.1.call-start = ((), (), s32[]{:S(2)}) async-start(), calls=%async_computation.2 | async-start | bytes 2621440 | tf_op jit(solution)/shard_map/reduce_scatter | solution.py:153
Sparse Core Ops, SparseCore 0:
  62.2 145.3 all-gather.1
  259.0 55.6 reduce-scatter.1
where the time goes:
time: 324 us; the launch traced here: 323 us
  blocking collectives  155 us (48%)
  local copies, waits for them, and re-layouts  61.7 us (19%)
  waiting for transfers between devices  56.3 us (17%)
  matrix products  14.5 us (4%)
  between operations  14.2 us (4%)
  other arithmetic  13.9 us (4%)
  starting transfers between devices  6 us (2%)
    all_gather x1, blocking collectives, local(): starts_in = lax.all_gather(band_start, 'tile', axis=0, tiled=True)  74.4 us
    reduce_scatter x1, waiting for transfers between devices, local(): lax.psum_scatter(partial_image, 'pulse', scatter_dimension=0, tiled=True)  55.8 us
    all_gather x1, blocking collectives, local(): flags_in = lax.all_gather(visible, 'tile', axis=0, tiled=True)  53.7 us
    unnamed x1, blocking collectives  26.6 us
    another operation x68, local copies, waits for them, and re-layouts, toeplitz_block(): repeated = jnp.tile(segment, block_width)[:2 * block_width * block_width]  21.6 us
    reshape x1, local copies, waits for them, and re-layouts, select_bands(): pieces = signals.reshape(pulses, 2, block_total, line_block)  14.6 us
    dot_general x17, matrix products, add_turn(): return running + jnp.dot(window, matrix, preferred_element_type=jnp.float32)  6.84 us
  transfers between devices with their start and end apart: 4, of which 2 were waited for; matrix products, arithmetic and copies ran while one was open for 3% of the time, Pallas kernels for 0%

commit v1 on v0

--- a/solution.py
+++ b/solution.py
@@ -134,7 +134,9 @@
     empty_index = jnp.zeros((group_pulses,), jnp.int32)
     first_row = jnp.int32(0)
     signals = lax.all_gather(compressed, "tile", axis=0, tiled=True)
-    starts_in = lax.all_gather(band_start, "tile", axis=0, tiled=True)
+    starts_in = jnp.concatenate(
+        lax.all_to_all(jnp.stack([band_start] * lax.axis_size("tile")), "tile", 0, 0), axis=0
+    )
     flags_in = lax.all_gather(visible, "tile", axis=0, tiled=True)
     doppler_in = lax.all_gather(doppler, "tile", axis=0, tiled=True)
     steps_in = lax.all_gather(range_step, "tile", axis=0, tiled=True)

time: 324 us -> 300 us (0.926)
  blocking collectives: 155 us -> 87.1 us
  waiting for transfers between devices: 56.3 us -> 82.2 us
  starting transfers between devices: 6 us -> 25.7 us
  local copies, waits for them, and re-layouts: 61.7 us -> 58.2 us
    all_gather x1 -> x0, blocking collectives: 74.4 us -> none  [local(): starts_in = lax.all_gather(band_start, 'tile', axis=0, tiled=True)]
    all_gather x1, waiting for transfers between devices: 0.02 us -> 29.2 us  [local(): signals = lax.all_gather(compressed, 'tile', axis=0, tiled=True)]
    all_to_all x0 -> x1, starting transfers between devices: none -> 19.7 us  [local(): lax.all_to_all(jnp.stack([band_start] * lax.axis_size('tile')), 'tile', 0...]
    all_gather x1, blocking collectives: 53.7 us -> 64.1 us  [local(): flags_in = lax.all_gather(visible, 'tile', axis=0, tiled=True)]
    dynamic_slice x1 -> x0, local copies, waits for them, and re-layouts: 4.96 us -> none  [local(): lax.dynamic_index_in_dim(starts_in[:, :, 0], tile_number, 1, keepdims=False)]
    unnamed x1, blocking collectives: 26.6 us -> 22.9 us
    reduce_scatter x1, waiting for transfers between devices: 55.8 us -> 52.5 us  [local(): lax.psum_scatter(partial_image, 'pulse', scatter_dimension=0, tiled=True)]
  transfers between devices with their start and end apart: 4 -> 5, of which waited for: 2 -> 3; matrix products, arithmetic and copies ran while one was open for 3% -> 2% of each run, Pallas kernels for 0% -> 0%
where the time goes in v1:
time: 300 us; the launch traced here: 299 us
  blocking collectives  87.1 us (29%)
  waiting for transfers between devices  82.2 us (27%)
  local copies, waits for them, and re-layouts  58.2 us (19%)
  starting transfers between devices  25.7 us (9%)
  other arithmetic  14.8 us (5%)
  matrix products  14.5 us (5%)
  between operations  14.4 us (5%)
    all_gather x1, blocking collectives, local(): flags_in = lax.all_gather(visible, 'tile', axis=0, tiled=True)  64.1 us
    reduce_scatter x1, waiting for transfers between devices, local(): lax.psum_scatter(partial_image, 'pulse', scatter_dimension=0, tiled=True)  52.5 us
    all_gather x1, waiting for transfers between devices, local(): signals = lax.all_gather(compressed, 'tile', axis=0, tiled=True)  29.2 us
    unnamed x1, blocking collectives  22.9 us
    another operation x68, local copies, waits for them, and re-layouts, toeplitz_block(): repeated = jnp.tile(segment, block_width)[:2 * block_width * block_width]  21.6 us
    all_to_all x1, starting transfers between devices, local(): lax.all_to_all(jnp.stack([band_start] * lax.axis_size('tile')), 'tile', 0...  19.7 us
    reshape x1, local copies, waits for them, and re-layouts, select_bands(): pieces = signals.reshape(pulses, 2, block_total, line_block)  14.6 us
    dot_general x17, matrix products, add_turn(): return running + jnp.dot(window, matrix, preferred_element_type=jnp.float32)  6.84 us
  transfers between devices with their start and end apart: 5, of which 3 were waited for; matrix products, arithmetic and copies ran while one was open for 2% of the time, Pallas kernels for 0%

profile of v1, /device:TPU:1, one launch (start us, length us, event | category | flops | bytes accessed | tf_op | source)
XLA Modules:
  0.0 298.9 jit_solution(12717202278375032453)
XLA Ops:
  6.5 0.9 fusion.50
  7.5 1.3 collective-permute-start.1
  8.8 4.7 %collective-permute-start = (bf16[2,8,2048]{2,1,0:T(8,128)(2,1)S(1)}, bf16[2,8,2048]{2,1,0:T(8,128)(2,1)S(1)}, u32[]{:S(2)}, u32[]{:S(2)}) collective-permute-start(bf16[2,8,2048]{2,1,0:T(8,128)(2,1)S(1)} %get-tuple-element.126), channel_id=1, source_target_pairs={{0,32},{32,64},{64,96},{1,33},{33,65},{65,97},{2,34},{34,66},{66,9... | collective-permute-start | bytes 196616 | tf_op jit(solution)/shard_map/ppermute | solution.py:18
  13.5 0.7 maximum_maximum_fusion
  14.8 1.0 pad_maximum_fusion.1
  15.8 45.2 %while.14 = (s32[]{:T(128)}, f32[256,512]{1,0:T(8,128)S(1)}, bf16[8,48,2,256]{3,1,0,2:T(8,128)(2,1)S(1)}, bf16[2,4609]{1,0:T(2,128)(2,1)S(1)}, s32[]{:T(128)}, /*index=5*/s32[]{:T(128)}, s32[]{:T(128)}, s32[]{:T(128)}) while((s32[]{:T(128)}, f32[256,512]{1,0:T(8,128)S(1)}, bf16[8,48,2,256]{3,1,0,2:T(8,128)(2,1)S(1)}, ...), condition=%wide.region_1.0_spmd.clone, body=%wide.region_0.0_spmd.clone.sunk | while | flops 136642560 | bytes 7779505 | solution.py:59
  16.4 0.6 tile.65
  17.2 0.6 tile.67
  19.0 0.6 tile.65
  19.9 0.6 tile.67
  21.7 0.6 tile.65
  22.6 0.6 tile.67
  24.4 0.6 tile.65
  25.2 0.6 tile.67
  27.0 0.6 tile.65
  27.9 0.6 tile.67
  29.7 0.6 tile.65
  30.5 0.6 tile.67
  32.3 0.6 tile.65
  33.2 0.6 tile.67
  35.0 0.6 tile.65
  35.9 0.6 tile.67
  37.7 0.6 tile.65
  43.0 0.6 tile.65
  43.8 0.6 tile.67
  45.6 0.6 tile.65
  49.2 0.6 tile.67
  51.0 0.6 tile.65
  51.8 0.6 tile.67
  57.1 0.6 tile.67
  58.9 0.6 tile.65
  61.3 0.8 convert_element_type.58
  62.1 0.7 reshape.227
  62.8 19.7 %all-to-all-start = ((s32[32,1,256]{2,1,0:T(1,128)}), s32[32,1,256]{2,1,0:T(1,128)S(1)}, u32[]{:S(2)}, u32[]{:S(2)}) async-start(s32[32,1,256]{2,1,0:T(1,128)} %reshape.227), calls=%async_computation | async-start | bytes 65536 | tf_op jit(solution)/shard_map/all_to_all | solution.py:138
  82.6 1.3 dynamic-slice.6
  85.1 22.9 %all-reduce.2 = (s32[256]{0:T(256)S(1)}, s32[256]{0:T(256)S(1)}) all-reduce(s32[256]{0:T(256)S(1)} %dynamic-update-slice.1, s32[256]{0:T(256)S(1)} %dynamic-update-slice), channel_id=1, replica_groups=mesh['pulse'=4,'range'=4,'tile'=32] {'tile'}, use_global_device_ids=true, to_apply=%add.1 | all-reduce | flops 512 | bytes 4096
  108.0 64.1 %all_gather.13 = s32[256,32]{1,0:T(8,128)S(1)} all-gather(s32[8,32]{1,0:T(8,128)S(1)} %copy-done.2), channel_id=1, replica_groups=mesh['pulse'=4,'range'=4,'tile'=32] {'tile'}, dimensions={0}, use_global_device_ids=true | all-gather | bytes 33792 | tf_op jit(solution)/shard_map/all_gather | solution.py:140
  172.3 1.3 multiply_convert_fusion.1
  174.2 0.7 reduce.8
  175.3 29.2 %all-gather.2.cloned.1.call-done = bf16[256,2,8192]{2,1,0:T(2,128)(2,1)} async-done(((bf16[8,2,8192]{2,1,0:T(2,128)(2,1)}), bf16[256,2,8192]{2,1,0:T(2,128)(2,1)}) %all-gather.2.cloned.1.call-update) | async-done | bytes 8388624 | tf_op jit(solution)/shard_map/all_gather | solution.py:136
  204.5 14.6 %reshape.204 = bf16[256,2,64,128]{3,2,1,0:T(8,128)(2,1)} reshape(bf16[256,2,8192]{2,1,0:T(2,128)(2,1)} %all-gather.2.cloned.1.call-done) | data formatting | bytes 16777216 | tf_op jit(solution)/shard_map/reshape | solution.py:68
  219.1 4.2 %convert_bitcast_fusion = bf16[256,2,9,128]{3,2,1,0:T(8,128)(2,1)S(1)} fusion(bf16[256,2,64,128]{3,2,1,0:T(8,128)(2,1)} %reshape.204, s32[256,9]{1,0:T(8,128)S(1)} %iota_add_fusion), kind=kOutput, calls=%fused_computation.26 | convolution fusion | flops 76234752 | bytes 9577472 | tf_op jit(solution)/shard_map/pjk,pckl->pcjl/dot_general | solution.py:73
  224.0 1.3 fusion.24
  225.5 5.1 %fusion.31 = bf16[256,1024]{0,1:T(8,128)(2,1)S(1)} fusion(f32[256,2,1024]{0,2,1:T(8,128)S(1)} %bitcast.78, s32[1024]{0:T(1024)S(1)} %iota_add_fusion.1, s32[256]{0:T(256)S(1)} %get-tuple-element.116), kind=kLoop, calls=%fused_computation.42 | loop fusion | flops 4718592 | bytes 2626560 | tf_op jit(solution)/shard_map/squeeze | solution.py:108
  230.6 5.1 %fusion.46 = (bf16[256,1024]{0,1:T(8,128)(2,1)S(1)}, bf16[256,1024]{0,1:T(8,128)(2,1)S(1)}) fusion(f32[256,2,1024]{0,2,1:T(8,128)S(1)} %bitcast.79, s32[1024]{0:T(1024)S(1)} %iota_add_fusion.1, s32[256]{0:T(256)S(1)} %get-tuple-element.116), kind=kLoop, calls=%fused_computation.78 | loop fusion | flops 5505024 | bytes 3150848 | tf_op jit(solution)/shard_map/neg | solution.py:111
  235.7 2.1 fusion.9
  237.8 52.5 %reduce-scatter.2.cloned.1.call-done = f32[64,2048]{1,0:T(8,128)} async-done(((f32[256,2048]{1,0:T(8,128)}), f32[64,2048]{1,0:T(8,128)}) %reduce-scatter.2.cloned.1.call-update) | async-done | bytes 524304 | tf_op jit(solution)/shard_map/reduce_scatter | solution.py:155
  290.2 1.9 copy.49
  (304 shorter events, 31.2 us)
Async XLA Ops:
  6.5 217.5 %copy-start = (bf16[8,256,128]{2,1,0:T(8,128)(2,1)S(1)}, bf16[8,256,128]{2,1,0:T(8,128)(2,1)}, u32[]{:S(2)}) copy-start(bf16[8,256,128]{2,1,0:T(8,128)(2,1)} %param.11) | copy-start | bytes 1572868
  6.5 198.0 %all-gather.2.cloned.1.call-start = ((), (), s32[]{:S(2)}) async-start(), calls=%async_computation.2 | async-start | bytes 8650752 | tf_op jit(solution)/shard_map/all_gather | solution.py:136
  7.5 6.8 %collective-permute-start.1 = (bf16[2,8,2048]{2,1,0:T(8,128)(2,1)S(1)}, bf16[2,8,2048]{2,1,0:T(8,128)(2,1)S(1)}, u32[]{:S(2)}, u32[]{:S(2)}) collective-permute-start(bf16[2,8,2048]{2,1,0:T(8,128)(2,1)S(1)} %get-tuple-element.127), channel_id=1, source_target_pairs={{32,0},{64,32},{96,64},{33,1},{65,33},{97,65},{34,2},{66,34},{98,6... | collective-permute-start | bytes 196616 | tf_op jit(solution)/shard_map/ppermute | solution.py:20
  8.8 6.0 %collective-permute-start = (bf16[2,8,2048]{2,1,0:T(8,128)(2,1)S(1)}, bf16[2,8,2048]{2,1,0:T(8,128)(2,1)S(1)}, u32[]{:S(2)}, u32[]{:S(2)}) collective-permute-start(bf16[2,8,2048]{2,1,0:T(8,128)(2,1)S(1)} %get-tuple-element.126), channel_id=1, source_target_pairs={{0,32},{32,64},{64,96},{1,33},{33,65},{65,97},{2,34},{34,66},{66,9... | collective-permute-start | bytes 196616 | tf_op jit(solution)/shard_map/ppermute | solution.py:18
  61.1 1.0 copy-start.1
  61.1 23.5 %copy-start.3 = (s32[8]{0:T(128)S(1)}, s32[8]{0:T(128)}, u32[]{:S(2)}) copy-start(s32[8]{0:T(128)} %param.15) | copy-start | bytes 100
  61.1 23.8 %copy-start.4 = (s32[8]{0:T(128)S(1)}, s32[8]{0:T(128)}, u32[]{:S(2)}) copy-start(s32[8]{0:T(128)} %param.14) | copy-start | bytes 100
  61.1 46.9 %copy-start.2 = (s32[8,32]{1,0:T(8,128)S(1)}, s32[8,32]{1,0:T(8,128)}, u32[]{:S(2)}) copy-start(s32[8,32]{1,0:T(8,128)} %param.13) | copy-start | bytes 3076
  62.8 110.8 %all-to-all-start = ((s32[32,1,256]{2,1,0:T(1,128)}), s32[32,1,256]{2,1,0:T(1,128)S(1)}, u32[]{:S(2)}, u32[]{:S(2)}) async-start(s32[32,1,256]{2,1,0:T(1,128)} %reshape.227), calls=%async_computation | async-start | bytes 65536 | tf_op jit(solution)/shard_map/all_to_all | solution.py:138
  82.5 207.7 %reduce-scatter.2.cloned.1.call-start = ((), (), s32[]{:S(2)}) async-start(), calls=%async_computation.3 | async-start | bytes 2621440 | tf_op jit(solution)/shard_map/reduce_scatter | solution.py:155
Sparse Core Ops, SparseCore 0:
  62.2 142.2 all-gather.1
  237.9 52.2 reduce-scatter.1
